TPU v7x, 32 devices: a whole 2x2x4 slice. The times are simulated.
32 devices in a mesh: seq: 4 (over y, x), fsdp: 8 (over z, core).
Axes of the slice: x: 2, y: 2, z: 4, core: 2. Of those that a mesh axis runs over, the one named last changes fastest.
Arguments:
- block_input: bfloat16 [8, 2048, 1024], P('fsdp', 'seq'), may hold values from -6 to 6
- norm_gain_a: float32 [1024], P('fsdp'), may hold values from 0.1 to 1.9
- weight_qkv: float32 [1024, 3072], P('fsdp'), may hold values from -0.1875 to 0.1875
- weight_out: float32 [1024, 1024], P('fsdp'), may hold values from -3 to 3
- norm_gain_b: float32 [1024], P('fsdp'), may hold values from 0.1 to 1.9
- weight_gate_up: float32 [1024, 8192], P('fsdp'), may hold values from -0.1875 to 0.1875
- weight_down: float32 [1024, 4096], P('fsdp'), may hold values from -0.09375 to 0.09375
- cotangent: bfloat16 [8, 2048, 1024], P('fsdp', 'seq'), may hold values from -6 to 6
- permutation: int32 [8, 2048], P('fsdp'), may hold values from 0 to 2047, each once within a row
- lengths: int32 [8, 3], P('fsdp'), may hold values from 256 to 1024, as said below
- offsets: int32 [8, 3], P('fsdp'), may hold values from 0 to 1792, as said below
Outputs:
- block_output: bfloat16 [8, 2048, 1024], P('fsdp', 'seq')
- grad_input: bfloat16 [8, 2048, 1024], P('fsdp', 'seq')
- grad_gain_a: float32 [1024], P('fsdp')
- grad_qkv: float32 [1024, 3072], P('fsdp')
- grad_out: float32 [1024, 1024], P('fsdp')
- grad_gain_b: float32 [1024], P('fsdp')
- grad_gate_up: float32 [1024, 8192], P('fsdp')
- grad_down: float32 [1024, 4096], P('fsdp')
Inputs may be any that keep to these rules, and one draw needn't show every extreme that they name: A group's 3 lengths sum to 2048, and its longest is exactly 1024. offsets[g, k] is the sum of lengths[g, i] over i < k, so that a group's sequences tile its positions.
All inputs are finite; a program needn't handle non-finite values.
Results may differ from a plain program's by a relative error of at most 0.02.
Values may be sent and summed in bfloat16 or wider, within the bound.
A program may use at most 256 MiB of HBM per device.

v0:
```python
import jax
import jax.numpy as jnp
from jax import lax
from jax.sharding import PartitionSpec as P

HEADS = 16
HEAD_DIM = 64
epsilon = 1e-05


def rms_scale(values):
    return lax.rsqrt(jnp.mean(values * values, axis=-1, keepdims=True) + epsilon)


def norm_backward(values, inv_scale, grad_normed, gain):
    scaled = grad_normed * gain
    gain_grad = jnp.sum(grad_normed * values * inv_scale, axis=0)
    input_grad = inv_scale * scaled - values * inv_scale**3 * jnp.mean(
        values * scaled, axis=-1, keepdims=True
    )
    return (input_grad, gain_grad)


def block_mask(seg_query, pos_query, segment, position):
    return (seg_query[:, None] == segment[None, :]) & (position[None, :] <= pos_query[:, None])


def on_device(
    block_input,
    norm_gain_a,
    weight_qkv,
    weight_out,
    norm_gain_b,
    weight_gate_up,
    weight_down,
    cotangent,
    permutation,
    lengths,
    offsets,
):
    seq_count = lax.axis_size("seq")
    row_count = block_input.shape[1]
    model_width = block_input.shape[2]
    group_len = row_count * seq_count
    head_local = HEADS // seq_count
    score_scale = HEAD_DIM ** (-0.5)
    blk_rows = min(512, group_len)
    block_count = group_len // blk_rows
    inputs = block_input[0].astype(jnp.float32)
    gain_a, full_qkv, full_out = (
        lax.all_gather(norm_gain_a.astype(jnp.bfloat16), "fsdp", axis=0, tiled=True),
        lax.all_gather(weight_qkv.astype(jnp.bfloat16), "fsdp", axis=0, tiled=True),
        lax.all_gather(weight_out.astype(jnp.bfloat16), "fsdp", axis=0, tiled=True),
    )
    inv_first = rms_scale(inputs)
    normed_a = (inputs * inv_first * gain_a.astype(jnp.float32)).astype(jnp.bfloat16)
    qkv_rows = jnp.dot(normed_a, full_qkv, preferred_element_type=jnp.float32).astype(jnp.bfloat16)
    head_rows = lax.all_to_all(
        qkv_rows.reshape(row_count, 3, seq_count, -1),
        "seq",
        split_axis=2,
        concat_axis=0,
        tiled=True,
    )
    head_rows = head_rows.reshape(group_len, 3, head_local, HEAD_DIM)
    position = jnp.arange(group_len, dtype=jnp.int32)
    dealt_pos = permutation[0]
    inverse = jnp.zeros((group_len,), jnp.int32).at[dealt_pos].set(position)
    ordered = head_rows[inverse]
    seq_starts = offsets[0]
    seq_lengths = lengths[0]
    inside = (position[:, None] >= seq_starts[None, :]) & (
        position[:, None] < seq_starts[None, :] + seq_lengths[None, :]
    )
    segment = jnp.sum(
        inside.astype(jnp.int32) * jnp.arange(seq_lengths.shape[0], dtype=jnp.int32)[None, :],
        axis=1,
    )
    queries = ordered[:, 0]
    key_rows = ordered[:, 1]
    values = ordered[:, 2]

    def forward_block(block_item):
        query_blk, seg_blk, pos_blk = block_item
        scores = (
            jnp.einsum("qhd,khd->hqk", query_blk, key_rows, preferred_element_type=jnp.float32)
            * score_scale
        )
        allowed = block_mask(seg_blk, pos_blk, segment, position)
        scores = jnp.where(allowed[None], scores, -1e30)
        row_top = jnp.max(scores, axis=-1, keepdims=True)
        exponent = jnp.exp(scores - row_top)
        row_total = jnp.sum(exponent, axis=-1, keepdims=True)
        weights_low = (exponent / row_total).astype(jnp.bfloat16)
        attended = jnp.einsum(
            "hqk,khd->qhd", weights_low, values, preferred_element_type=jnp.float32
        )
        return (attended.astype(jnp.bfloat16), (row_top + jnp.log(row_total))[:, :, 0])

    query_blocks = queries.reshape(block_count, blk_rows, head_local, HEAD_DIM)
    seg_blocks = segment.reshape(block_count, blk_rows)
    pos_blocks = position.reshape(block_count, blk_rows)
    attended, log_total = lax.map(forward_block, (query_blocks, seg_blocks, pos_blocks))
    dealt_out = attended.reshape(group_len, -1)[dealt_pos]
    mixed = lax.all_to_all(
        dealt_out.reshape(group_len, 1, -1), "seq", split_axis=0, concat_axis=1, tiled=True
    ).reshape(row_count, model_width)
    hidden = inputs + jnp.dot(mixed, full_out, preferred_element_type=jnp.float32)
    gain_b, full_gate_up, full_down = (
        lax.all_gather(norm_gain_b.astype(jnp.bfloat16), "fsdp", axis=0, tiled=True),
        lax.all_gather(weight_gate_up.astype(jnp.bfloat16), "fsdp", axis=0, tiled=True),
        lax.all_gather(weight_down.astype(jnp.bfloat16), "fsdp", axis=0, tiled=True),
    )
    inv_second = rms_scale(hidden)
    normed_b = (hidden * inv_second * gain_b.astype(jnp.float32)).astype(jnp.bfloat16)
    gate_up = jnp.dot(normed_b, full_gate_up, preferred_element_type=jnp.float32)
    hidden_units = full_gate_up.shape[1] // 2
    gate_part = gate_up[:, :hidden_units]
    up_part = gate_up[:, hidden_units:]
    gate_sigmoid = jax.nn.sigmoid(gate_part)
    gate_silu = gate_part * gate_sigmoid
    activation = (gate_silu * up_part).astype(jnp.bfloat16)
    branch_out = jnp.einsum("rf,df->rd", activation, full_down, preferred_element_type=jnp.float32)
    result_rows = (hidden + branch_out).astype(jnp.bfloat16)
    gain_b, full_gate_up, full_down = (
        lax.all_gather(norm_gain_b.astype(jnp.bfloat16), "fsdp", axis=0, tiled=True),
        lax.all_gather(weight_gate_up.astype(jnp.bfloat16), "fsdp", axis=0, tiled=True),
        lax.all_gather(weight_down.astype(jnp.bfloat16), "fsdp", axis=0, tiled=True),
    )
    out_grad = cotangent[0].astype(jnp.float32)
    out_grad_low = out_grad.astype(jnp.bfloat16)
    grad_down_term = jnp.einsum(
        "rd,rf->df", out_grad_low, activation, preferred_element_type=jnp.float32
    )
    grad_activation = jnp.dot(out_grad_low, full_down, preferred_element_type=jnp.float32)
    grad_gate = grad_activation * up_part * gate_sigmoid * (1.0 + gate_part * (1.0 - gate_sigmoid))
    grad_up = grad_activation * gate_silu
    grad_gate_up = jnp.concatenate([grad_gate, grad_up], axis=1).astype(jnp.bfloat16)
    grad_gate_up_term = jnp.einsum(
        "rd,rf->df", normed_b, grad_gate_up, preferred_element_type=jnp.float32
    )
    grad_normed_b = jnp.einsum(
        "rf,df->rd", grad_gate_up, full_gate_up, preferred_element_type=jnp.float32
    )
    hidden_back, grad_gain_b_term = norm_backward(
        hidden, inv_second, grad_normed_b, gain_b.astype(jnp.float32)
    )
    grad_hidden = out_grad + hidden_back
    gain_a, full_qkv, full_out = (
        lax.all_gather(norm_gain_a.astype(jnp.bfloat16), "fsdp", axis=0, tiled=True),
        lax.all_gather(weight_qkv.astype(jnp.bfloat16), "fsdp", axis=0, tiled=True),
        lax.all_gather(weight_out.astype(jnp.bfloat16), "fsdp", axis=0, tiled=True),
    )
    grad_branch = grad_hidden.astype(jnp.bfloat16)
    grad_out_term = jnp.einsum("rd,re->de", mixed, grad_branch, preferred_element_type=jnp.float32)
    grad_mixed = jnp.einsum(
        "re,de->rd", grad_branch, full_out, preferred_element_type=jnp.float32
    ).astype(jnp.bfloat16)
    grad_heads = lax.all_to_all(
        grad_mixed.reshape(row_count, seq_count, -1), "seq", split_axis=1, concat_axis=0, tiled=True
    )
    grad_ordered = grad_heads.reshape(group_len, head_local, HEAD_DIM)[inverse]
    grad_blocks = grad_ordered.reshape(block_count, blk_rows, head_local, HEAD_DIM)

    def backward_block(carry, block_item):
        key_acc, value_acc = carry
        query_blk, grad_blk, log_blk, seg_blk, pos_blk = block_item
        scores = (
            jnp.einsum("qhd,khd->hqk", query_blk, key_rows, preferred_element_type=jnp.float32)
            * score_scale
        )
        allowed = block_mask(seg_blk, pos_blk, segment, position)
        scores = jnp.where(allowed[None], scores, -1e30)
        probability = jnp.exp(scores - log_blk[:, :, None])
        grad_prob = jnp.einsum("qhd,khd->hqk", grad_blk, values, preferred_element_type=jnp.float32)
        row_delta = jnp.sum(probability * grad_prob, axis=-1, keepdims=True)
        grad_score = (probability * (grad_prob - row_delta)).astype(jnp.bfloat16)
        grad_query = (
            jnp.einsum("hqk,khd->qhd", grad_score, key_rows, preferred_element_type=jnp.float32)
            * score_scale
        )
        key_acc = (
            key_acc
            + jnp.einsum("hqk,qhd->khd", grad_score, query_blk, preferred_element_type=jnp.float32)
            * score_scale
        )
        value_acc = value_acc + jnp.einsum(
            "hqk,qhd->khd",
            probability.astype(jnp.bfloat16),
            grad_blk,
            preferred_element_type=jnp.float32,
        )
        return ((key_acc, value_acc), grad_query.astype(jnp.bfloat16))

    zero_acc = jnp.zeros((group_len, head_local, HEAD_DIM), jnp.float32)
    accumulated, query_grad = lax.scan(
        backward_block,
        (zero_acc, zero_acc),
        (query_blocks, grad_blocks, log_total, seg_blocks, pos_blocks),
    )
    qkv_grad = jnp.stack(
        [
            query_grad.reshape(group_len, -1),
            accumulated[0].reshape(group_len, -1).astype(jnp.bfloat16),
            accumulated[1].reshape(group_len, -1).astype(jnp.bfloat16),
        ],
        axis=1,
    )
    dealt_grad = qkv_grad[dealt_pos]
    rows_grad = lax.all_to_all(
        dealt_grad.reshape(group_len, 3, 1, -1), "seq", split_axis=0, concat_axis=2, tiled=True
    ).reshape(row_count, -1)
    grad_qkv_term = jnp.einsum("rd,re->de", normed_a, rows_grad, preferred_element_type=jnp.float32)
    grad_normed_a = jnp.einsum("re,de->rd", rows_grad, full_qkv, preferred_element_type=jnp.float32)
    input_back, grad_gain_a_term = norm_backward(
        inputs, inv_first, grad_normed_a, gain_a.astype(jnp.float32)
    )
    input_grad = (grad_hidden + input_back).astype(jnp.bfloat16)
    attn_shards = (
        lax.psum_scatter(
            grad_gain_a_term.astype(jnp.bfloat16), "fsdp", scatter_dimension=0, tiled=True
        ).astype(jnp.float32),
        lax.psum_scatter(
            grad_qkv_term.astype(jnp.bfloat16), "fsdp", scatter_dimension=0, tiled=True
        ).astype(jnp.float32),
        lax.psum_scatter(
            grad_out_term.astype(jnp.bfloat16), "fsdp", scatter_dimension=0, tiled=True
        ).astype(jnp.float32),
    )
    mlp_shards = (
        lax.psum_scatter(
            grad_gain_b_term.astype(jnp.bfloat16), "fsdp", scatter_dimension=0, tiled=True
        ).astype(jnp.float32),
        lax.psum_scatter(
            grad_gate_up_term.astype(jnp.bfloat16), "fsdp", scatter_dimension=0, tiled=True
        ).astype(jnp.float32),
        lax.psum_scatter(
            grad_down_term.astype(jnp.bfloat16), "fsdp", scatter_dimension=0, tiled=True
        ).astype(jnp.float32),
    )
    totals = (
        lax.psum(attn_shards[0].astype(jnp.bfloat16), "seq").astype(jnp.float32),
        lax.psum(attn_shards[1].astype(jnp.bfloat16), "seq").astype(jnp.float32),
        lax.psum(attn_shards[2].astype(jnp.bfloat16), "seq").astype(jnp.float32),
        lax.psum(mlp_shards[0].astype(jnp.bfloat16), "seq").astype(jnp.float32),
        lax.psum(mlp_shards[1].astype(jnp.bfloat16), "seq").astype(jnp.float32),
        lax.psum(mlp_shards[2].astype(jnp.bfloat16), "seq").astype(jnp.float32),
    )
    return (
        result_rows[None],
        input_grad[None],
        totals[0],
        totals[1],
        totals[2],
        totals[3],
        totals[4],
        totals[5],
    )


def solution(mesh):
    placed = (
        P("fsdp", "seq", None),
        P("fsdp"),
        P("fsdp", None),
        P("fsdp", None),
        P("fsdp"),
        P("fsdp", None),
        P("fsdp", None),
        P("fsdp", "seq", None),
        P("fsdp", None),
        P("fsdp", None),
        P("fsdp", None),
    )
    return jax.shard_map(
        on_device,
        mesh=mesh,
        in_specs=placed,
        out_specs=(
            P("fsdp", "seq", None),
            P("fsdp", "seq", None),
            P("fsdp"),
            P("fsdp", None),
            P("fsdp", None),
            P("fsdp"),
            P("fsdp", None),
            P("fsdp", None),
        ),
        check_vma=False,
    )
```

profile of v0, /device:TPU:0, one launch (start us, length us, event | category | flops | bytes accessed | tf_op | source)
XLA Modules:
  0.0 1127.1 jit_solution(276207675843231154)
XLA Ops:
  15.4 13.5 %all-gather = bf16[8,1,128]{2,1,0:T(2,128)(2,1)S(1)} all-gather(bf16[1,1,128]{2,1,0:T(2,128)(2,1)S(1)} %convert_bitcast_fusion.3), channel_id=1, replica_groups=mesh['seq'=4,'fsdp'=8] {'fsdp'}, dimensions={0}, use_global_device_ids=true | all-gather | bytes 2304 | tf_op jit(solution)/shard_map/all_gather | solution.py:51
  29.8 47.9 %all-gather.7.cloned.1.call-done = bf16[1024,3072]{1,0:T(8,128)(2,1)} async-done(((bf16[128,3072]{1,0:T(8,128)(2,1)}), bf16[1024,3072]{1,0:T(8,128)(2,1)}) %all-gather.7.cloned.1.call-update) | async-done | bytes 6291472 | tf_op jit(solution)/shard_map/all_gather | solution.py:52
  112.3 23.5 %all-to-all-done = bf16[512,3,4,256]{0,3,1,2:T(8,128)(2,1)S(1)} async-done(((bf16[512,3,4,256]{0,3,1,2:T(8,128)(2,1)}), bf16[512,3,4,256]{0,3,1,2:T(8,128)(2,1)S(1)}, u32[]{:S(2)}, u32[]{:S(2)}) %all-to-all-start) | async-done | bytes 3145760 | tf_op jit(solution)/shard_map/all_to_all | solution.py:58
  140.4 13.1 %reshape.380 = bf16[2048,3,4,64]{3,2,1,0:T(4,128)(2,1)} reshape(bf16[4,512,3,1,256]{4,2,1,0,3:T(4,128)(2,1)} %copy.141) | data formatting | bytes 6291456 | tf_op jit(solution)/shard_map/reshape | solution.py:65
  153.6 23.0 %gather_fusion = bf16[2048,3,4,64]{3,2,1,0:T(4,128)(2,1)} fusion(bf16[2048,3,4,64]{3,2,1,0:T(4,128)(2,1)} %reshape.380, s32[2048]{0:T(1024)S(1)} %fusion.84), kind=kCustom, calls=%fused_computation | custom fusion | bytes 6299648 | tf_op jit(solution)/shard_map/gather | solution.py:69
  191.8 64.2 %while.28 = (s32[]{:T(128)}, bf16[4,512,4,64]{1,3,2,0:T(8,128)(2,1)}, f32[4,4,512]{2,1,0:T(4,128)}, s32[4,512]{1,0:T(4,128)}, s32[2048]{0:T(1024)S(1)}, /*index=...) while((s32[]{:T(128)}, ...), condition=%wide.region_6.7_spmd.clone, body=%wide.region_3.6_spmd.clone.sunk | while | flops 1127348224 | bytes 57233532 | solution.py:103
  310.1 18.8 %fusion.89 = f32[512,8192]{1,0:T(8,128)} fusion(bf16[1024,8192]{1,0:T(8,128)(2,1)} %all-gather.11.cloned.1.call-done, f32[512,1024]{1,0:T(8,128)} %get-tuple-element.422, f32[1024]{0:T(1024)S(1)} %bitcast.234, f32[512]{0:T(512)S(1)} %get-tuple-element.420), kind=kOutput, calls=%fused_computation.139 | convolution fusion | flops 8591507456 | bytes 35657728 | tf_op jit(solution)/shard_map/dot_general | solution.py:116
  328.9 13.4 %all-gather.13.cloned.1.call-done = bf16[1024,4096]{1,0:T(8,128)(2,1)} async-done(((bf16[128,4096]{1,0:T(8,128)(2,1)}), bf16[1024,4096]{1,0:T(8,128)(2,1)}) %all-gather.13.cloned.1.call-update) | async-done | bytes 8388624 | tf_op jit(solution)/shard_map/all_gather | solution.py:112
  342.3 15.1 %multiply_convert_fusion.2 = (bf16[512,4096]{1,0:T(8,128)(2,1)}, bf16[512,4096]{1,0:T(8,128)(2,1)}, bf16[512,4096]{1,0:T(8,128)(2,1)S(1)}) fusion(f32[512,8192]{1,0:T(8,128)} %fusion.89, bf16[1024,4096]{1,0:T(8,128)(2,1)} %all-gather.13.cloned.1.call-done, bf16[1,512,1024]{2,1,0:T(8,128)(2,1)S(1)} %copy-done.22), kind=kOutput, calls=%fused_computation.67 | convolution fusion | flops 4326424576 | bytes 38797312 | tf_op jit(solution)/shard_map/dot_general | solution.py:135
  366.2 11.7 %copy.151 = bf16[1024,4096]{1,0:T(8,128)(2,1)} copy(bf16[1024,4096]{0,1:T(8,128)(2,1)} %convert_bitcast_fusion) | data formatting | bytes 16777216
  377.9 18.0 %multiply_reduce_fusion.1 = (bf16[1024]{0:T(1024)(128)(2,1)}, f32[512]{0:T(512)S(1)}, f32[512,1024]{1,0:T(8,128)}) fusion(f32[512,1024]{1,0:T(8,128)} %get-tuple-element.422, f32[512]{0:T(512)S(1)} %get-tuple-element.420, f32[1024]{0:T(1024)S(1)} %bitcast.235, bf16[1024,8192]{1,0:T(8,128)(2,1)} %all-gather.11.cloned.1.call-done, ...), kind=kOutput, calls=%fused_computation.97 | convolution fusion | flops 8609855488 | bytes 29370368 | tf_op jit(solution)/shard_map/rf,df->rd/dot_general | solution.py:142
  425.0 16.1 %gather_fusion.2 = bf16[2048,4,64]{2,1,0:T(4,128)(2,1)} fusion(bf16[2048,4,64]{2,1,0:T(4,128)(2,1)} %reshape.382, s32[2048]{0:T(1024)S(1)} %copy-done.27), kind=kCustom, calls=%fused_computation.2 | custom fusion | bytes 2105344 | tf_op jit(solution)/shard_map/gather | solution.py:162
  446.2 209.1 %while.29 = (s32[]{:T(128)}, f32[2048,4,64]{0,2,1:T(8,128)}, f32[2048,4,64]{0,2,1:T(8,128)}, bf16[4,512,4,64]{1,3,2,0:T(8,128)(2,1)}, bf16[4,512,4,64]{1,3,2,0:T...) while((s32[]{:T(128)}, f32[2048,4,64]{0,2,1:T(8,128)}, ...), condition=%wide.region_11.12_spmd.clone, body=%wide.region_9.11_spmd.clone.sunk | while | flops 2753296384 | bytes 268841472 | solution.py:196
  454.4 12.3 %multiply_reduce_fusion.5 = (f32[4,512]{1,0:T(4,128)}, f32[4,512,2048]{2,1,0:T(8,128)}) fusion(f32[4,512,2048]{2,1,0:T(8,128)S(1)} %fusion.146, f32[4,512]{1,0:T(4,128)S(1)} %dynamic-slice_bitcast_fusion.2, pred[512,2048]{1,0:T(8,128)(4,1)S(1)} %fusion.147, bf16[2048,4,64]{0,2,1:T(8,128)(2,1)} %get-tuple-element.638, ...), kind=kOutput, calls=%fused_computation.28.clone.1 | convolution fusion | flops 557840384 | bytes 35930116 | tf_op jit(solution)/shard_map/while/body/eval_jaxpr/qhd,khd->hqk/dot_general | solution.py:175
  506.3 12.3 %multiply_reduce_fusion.5 = (f32[4,512]{1,0:T(4,128)}, f32[4,512,2048]{2,1,0:T(8,128)}) fusion(f32[4,512,2048]{2,1,0:T(8,128)S(1)} %fusion.146, f32[4,512]{1,0:T(4,128)S(1)} %dynamic-slice_bitcast_fusion.2, pred[512,2048]{1,0:T(8,128)(4,1)S(1)} %fusion.147, bf16[2048,4,64]{0,2,1:T(8,128)(2,1)} %get-tuple-element.638, ...), kind=kOutput, calls=%fused_computation.28.clone.1 | convolution fusion | flops 557840384 | bytes 35930116 | tf_op jit(solution)/shard_map/while/body/eval_jaxpr/qhd,khd->hqk/dot_general | solution.py:175
  558.5 12.3 %multiply_reduce_fusion.5 = (f32[4,512]{1,0:T(4,128)}, f32[4,512,2048]{2,1,0:T(8,128)}) fusion(f32[4,512,2048]{2,1,0:T(8,128)S(1)} %fusion.146, f32[4,512]{1,0:T(4,128)S(1)} %dynamic-slice_bitcast_fusion.2, pred[512,2048]{1,0:T(8,128)(4,1)S(1)} %fusion.147, bf16[2048,4,64]{0,2,1:T(8,128)(2,1)} %get-tuple-element.638, ...), kind=kOutput, calls=%fused_computation.28.clone.1 | convolution fusion | flops 557840384 | bytes 35930116 | tf_op jit(solution)/shard_map/while/body/eval_jaxpr/qhd,khd->hqk/dot_general | solution.py:175
  610.7 12.3 %multiply_reduce_fusion.5 = (f32[4,512]{1,0:T(4,128)}, f32[4,512,2048]{2,1,0:T(8,128)}) fusion(f32[4,512,2048]{2,1,0:T(8,128)S(1)} %fusion.146, f32[4,512]{1,0:T(4,128)S(1)} %dynamic-slice_bitcast_fusion.2, pred[512,2048]{1,0:T(8,128)(4,1)S(1)} %fusion.147, bf16[2048,4,64]{0,2,1:T(8,128)(2,1)} %get-tuple-element.638, ...), kind=kOutput, calls=%fused_computation.28.clone.1 | convolution fusion | flops 557840384 | bytes 35930116 | tf_op jit(solution)/shard_map/while/body/eval_jaxpr/qhd,khd->hqk/dot_general | solution.py:175
  686.7 18.7 %gather_fusion.3 = bf16[2048,3,256]{2,1,0:T(4,128)(2,1)} fusion(bf16[2048,3,256]{2,1,0:T(4,128)(2,1)} %pad_maximum_fusion.3, s32[2048]{0:T(1024)S(1)} %copy-done.25), kind=kCustom, calls=%fused_computation.3 | custom fusion | bytes 6299648 | tf_op jit(solution)/shard_map/gather | solution.py:209
  705.4 51.5 %all_to_all.60 = bf16[2048,3,1,256]{3,1,2,0:T(4,128)(2,1)S(1)} all-to-all(bf16[2048,3,1,256]{3,1,2,0:T(4,128)(2,1)} %bitcast.213), channel_id=1, replica_groups=mesh['seq'=4,'fsdp'=8] {'seq'}, dimensions={0} | all-to-all | bytes 6291456 | tf_op jit(solution)/shard_map/all_to_all | solution.py:210
  770.4 16.6 %convolution_convert_fusion = bf16[1024,8192]{1,0:T(8,128)(2,1)} fusion(bf16[512,4096]{1,0:T(8,128)(2,1)} %get-tuple-element.412, bf16[512,4096]{1,0:T(8,128)(2,1)} %get-tuple-element.411, f32[512,1024]{1,0:T(8,128)S(1)} %copy-done.12, f32[1024]{0:T(1024)S(1)} %bitcast.237, f32[512]{0:T(512)S(1)} %copy-done.36), kind=kOutput, calls=%fused_computation.63 | convolution fusion | flops 8616673280 | bytes 27269120 | tf_op jit(solution)/shard_map/rd,rf->df/dot_general | solution.py:139
  789.6 45.9 %reduce-scatter.7.cloned.1.call-done = bf16[128,3072]{1,0:T(8,128)(2,1)} async-done(((bf16[1024,3072]{1,0:T(8,128)(2,1)}), bf16[128,3072]{1,0:T(8,128)(2,1)}) %reduce-scatter.7.cloned.1.call-update) | async-done | bytes 786448 | tf_op jit(solution)/shard_map/reduce_scatter | solution.py:223
  835.4 169.0 %reduce-scatter.11.cloned.1.call-done = bf16[128,8192]{1,0:T(8,128)(2,1)} async-done(((bf16[1024,8192]{1,0:T(8,128)(2,1)}), bf16[128,8192]{1,0:T(8,128)(2,1)}) %reduce-scatter.11.cloned.1.call-update) | async-done | bytes 2097168 | tf_op jit(solution)/shard_map/reduce_scatter | solution.py:234
  1024.0 13.6 %all-reduce.2 = (bf16[1024]{0:T(1024)(128)(2,1)S(1)}, bf16[1024]{0:T(1024)(128)(2,1)S(1)}) all-reduce(bf16[1024]{0:T(1024)(128)(2,1)S(1)} %get-tuple-element.351, bf16[1024]{0:T(1024)(128)(2,1)S(1)} %copy-done.38), channel_id=2, replica_groups=mesh['seq'=4,'fsdp'=8] {'fsdp'}, use_global_device_ids=true, to_apply=%region_14.15.clone | all-reduce | flops 2048 | bytes 8192
  1052.1 59.8 %all-reduce.7.cloned.1.call-done = (bf16[128,4096]{0,1:T(8,128)(2,1)}, bf16[128,3072]{1,0:T(8,128)(2,1)}, bf16[128,1024]{1,0:T(8,128)(2,1)}, bf16[128,8192]{1,0:T(8,128)(2,1)}) async-done(((bf16[128,4096]{0,1:T(8,128)(2,1)}, bf16[128,3072]{1,0:T(8,128)(2,1)}, bf16[128,1024]{1,0:T(8,128)(2,1)}, bf16[128,8192]{1,0:T(8,128)(2,1)}), (bf16[128,4096]{0,1:T(8,128)(2,1)}, bf16[128,3072]{1,0:T(8,128)(2,1)}, ...) | async-done | bytes 4194320 | tf_op jit(solution)/shard_map/psum | solution.py:247
  (325 shorter events, 472.4 us)
Async XLA Ops:
  7.2 70.6 %all-gather.7.cloned.1.call-start = ((), (), s32[]{:S(2)}) async-start(), calls=%async_computation.8 | async-start | bytes 7077888 | tf_op jit(solution)/shard_map/all_gather | solution.py:52
  9.6 295.9 %all-gather.9.cloned.1.call-start = ((), (), s32[]{:S(2)}) async-start(), calls=%async_computation.9 | async-start | bytes 2359296 | tf_op jit(solution)/shard_map/all_gather | solution.py:53
  11.5 17.4 %copy-start.7 = (bf16[1,512,1024]{2,1,0:T(8,128)(2,1)S(1)}, bf16[1,512,1024]{2,1,0:T(8,128)(2,1)}, u32[]{:S(2)}) copy-start(bf16[1,512,1024]{2,1,0:T(8,128)(2,1)} %param.15) | copy-start | bytes 3145732
  11.5 298.6 %all-gather.11.cloned.1.call-start = ((), (), s32[]{:S(2)}) async-start(), calls=%async_computation.10 | async-start | bytes 18874368 | tf_op jit(solution)/shard_map/all_gather | solution.py:111
  28.9 48.8 %copy-start.30 = (f32[8,1,128]{2,1,0:T(1,128)}, f32[8,1,128]{2,1,0:T(1,128)S(1)}, u32[]{:S(2)}) copy-start(f32[8,1,128]{2,1,0:T(1,128)S(1)} %convert_element_type.214) | copy-start | bytes 12292
  29.8 47.9 %copy-start.33 = (f32[512]{0:T(512)}, f32[512]{0:T(512)S(1)}, u32[]{:S(2)}) copy-start(f32[512]{0:T(512)S(1)} %get-tuple-element.418) | copy-start | bytes 6148
  95.2 40.6 %all-to-all-start = ((bf16[512,3,4,256]{0,3,1,2:T(8,128)(2,1)}), bf16[512,3,4,256]{0,3,1,2:T(8,128)(2,1)S(1)}, u32[]{:S(2)}, u32[]{:S(2)}) async-start(bf16[512,3,4,256]{0,3,1,2:T(8,128)(2,1)} %copy.114), calls=%async_computation | async-start | bytes 6291456 | tf_op jit(solution)/shard_map/all_to_all | solution.py:58
  99.1 243.2 %all-gather.13.cloned.1.call-start = ((), (), s32[]{:S(2)}) async-start(), calls=%async_computation.11 | async-start | bytes 9437184 | tf_op jit(solution)/shard_map/all_gather | solution.py:112
  112.3 41.2 %copy-start.26 = (s32[2048]{0:T(1024)}, s32[2048]{0:T(1024)S(1)}, u32[]{:S(2)}) copy-start(s32[2048]{0:T(1024)S(1)} %fusion.84) | copy-start | bytes 24580
  278.5 17.8 %all-to-all-start.1 = ((bf16[4,2,65536]{2,1,0:T(2,128)(2,1)}), bf16[4,2,65536]{2,1,0:T(2,128)(2,1)}, u32[]{:S(2)}, u32[]{:S(2)}) async-start(bf16[4,2,65536]{2,1,0:T(2,128)(2,1)} %reshape.393), calls=%async_computation.1 | async-start | bytes 2097152 | tf_op jit(solution)/shard_map/all_to_all | solution.py:105
  282.8 504.3 %reduce-scatter.13.cloned.1.call-start = ((), (), s32[]{:S(2)}) async-start(), calls=%async_computation.15 | async-start | bytes 9437184
  292.7 103.2 %copy-start.28 = (f32[8,1,128]{2,1,0:T(1,128)}, f32[8,1,128]{2,1,0:T(1,128)S(1)}, u32[]{:S(2)}) copy-start(f32[8,1,128]{2,1,0:T(1,128)S(1)} %convert_element_type.215) | copy-start | bytes 12292
  310.0 85.9 %copy-start.35 = (f32[512]{0:T(512)}, f32[512]{0:T(512)S(1)}, u32[]{:S(2)}) copy-start(f32[512]{0:T(512)S(1)} %get-tuple-element.420) | copy-start | bytes 6148
  310.1 32.2 %copy-start.22 = (bf16[1,512,1024]{2,1,0:T(8,128)(2,1)S(1)}, bf16[1,512,1024]{2,1,0:T(8,128)(2,1)}, u32[]{:S(2)}) copy-start(bf16[1,512,1024]{2,1,0:T(8,128)(2,1)} %param.22) | copy-start | bytes 3145732
  402.8 17.9 %all-to-all-start.2 = ((bf16[512,4,256]{0,2,1:T(8,128)(2,1)}), bf16[512,4,256]{0,2,1:T(8,128)(2,1)S(1)}, u32[]{:S(2)}, u32[]{:S(2)}) async-start(bf16[512,4,256]{0,2,1:T(8,128)(2,1)} %bitcast.222), calls=%async_computation.2 | async-start | bytes 2097152 | tf_op jit(solution)/shard_map/all_to_all | solution.py:159
  406.5 383.0 %reduce-scatter.9.cloned.1.call-start = ((), (), s32[]{:S(2)}) async-start(), calls=%async_computation.13 | async-start | bytes 2359296 | tf_op jit(solution)/shard_map/reduce_scatter | solution.py:226
  411.1 424.3 %reduce-scatter.7.cloned.1.call-start = ((), (), s32[]{:S(2)}) async-start(), calls=%async_computation.12 | async-start | bytes 7077888 | tf_op jit(solution)/shard_map/reduce_scatter | solution.py:223
  450.9 15.8 %copy-start = (f32[4,512,2048]{2,1,0:T(8,128)}, f32[4,512,2048]{2,1,0:T(8,128)S(1)}, u32[]{:S(2)}) copy-start(f32[4,512,2048]{2,1,0:T(8,128)S(1)} %fusion.146) | copy-start | bytes 50331652 | tf_op jit(solution)/shard_map/while
  607.2 15.8 %copy-start = (f32[4,512,2048]{2,1,0:T(8,128)}, f32[4,512,2048]{2,1,0:T(8,128)S(1)}, u32[]{:S(2)}) copy-start(f32[4,512,2048]{2,1,0:T(8,128)S(1)} %fusion.146) | copy-start | bytes 50331652 | tf_op jit(solution)/shard_map/while
  768.8 235.6 %reduce-scatter.11.cloned.1.call-start = ((), (), s32[]{:S(2)}) async-start(), calls=%async_computation.14 | async-start | bytes 18874368 | tf_op jit(solution)/shard_map/reduce_scatter | solution.py:234
  787.0 217.4 %copy-start.43 = (u32[32]{0:T(128)S(1)}, u32[32]{0:T(128)}, u32[]{:S(2)}) copy-start(u32[32]{0:T(128)} %constant.73) | copy-start | bytes 388
  787.0 324.9 %all-reduce.7.cloned.1.call-start = ((), (), s32[]{:S(2)}) async-start(), calls=%async_computation.16 | async-start | bytes 8388608 | tf_op jit(solution)/shard_map/psum | solution.py:247
  1016.0 33.0 %copy-start.11 = (f32[512,1024]{1,0:T(8,128)S(1)}, f32[512,1024]{1,0:T(8,128)}, u32[]{:S(2)}) copy-start(f32[512,1024]{1,0:T(8,128)} %copy-done.10) | copy-start | bytes 6291460
  1016.0 33.0 %copy-start.32 = (f32[512]{0:T(512)S(1)}, f32[512]{0:T(512)}, u32[]{:S(2)}) copy-start(f32[512]{0:T(512)} %get-tuple-element.417) | copy-start | bytes 6148
  (68 other events, 437.8 us)
Sparse Core Ops, SparseCore 0:
  10.2 67.4 all-gather.6
  79.9 27.7 all-gather.8
  109.3 150.5 all-gather.10
  261.9 80.2 all-gather.12
  378.0 88.1 reduce-scatter.12
  468.4 34.2 reduce-scatter.8
  768.9 66.4 reduce-scatter.6
  837.8 166.5 reduce-scatter.10
  1008.7 103.2 all-reduce.6
where the time goes:
time: 1140 us; the launch traced here: 1130 us
  waiting for transfers between devices  373 us (33%)
  matrix products  303 us (27%)
  local copies, waits for them, and re-layouts  207 us (18%)
  other arithmetic  117 us (10%)
  blocking collectives  98.6 us (9%)
  between operations  15.1 us (1%)
  starting transfers between devices  12.2 us (1%)
    reduce_scatter x1, waiting for transfers between devices, on_device(): lax.psum_scatter(grad_gate_up_term.astype(jnp.bfloat16), 'fsdp', scatter_...  169 us
    psum x1, waiting for transfers between devices, on_device(): lax.psum(mlp_shards[2].astype(jnp.bfloat16), 'seq').astype(jnp.float32)  59.8 us
    all_to_all x1, blocking collectives, on_device(): lax.all_to_all(dealt_grad.reshape(group_len, 3, 1, -1), 'seq', split_axis...  51.5 us
    dot_general x4, matrix products, backward_block(): jnp.einsum('qhd,khd->hqk', grad_blk, values, preferred_element_type=jnp.f...  49.3 us
    all_gather x1, waiting for transfers between devices, on_device(): lax.all_gather(weight_qkv.astype(jnp.bfloat16), 'fsdp', axis=0, tiled=True)  47.9 us
    reduce_scatter x1, waiting for transfers between devices, on_device(): lax.psum_scatter(grad_qkv_term.astype(jnp.bfloat16), 'fsdp', scatter_dime...  45.9 us
    unnamed x85, local copies, waits for them, and re-layouts  44.8 us
    convert_element_type x4, other arithmetic, backward_block(): grad_score = (probability * (grad_prob - row_delta)).astype(jnp.bfloat16)  43.7 us
  transfers between devices with their start and end apart: 12, of which 8 were waited for; matrix products, arithmetic and copies ran while one was open for 51% of the time, Pallas kernels for 0%

commit v1 on v0

--- a/solution.py
+++ b/solution.py
@@ -6,6 +6,17 @@
 HEADS = 16
 HEAD_DIM = 64
 epsilon = 1e-05
+
+
+def cut_along(value, dim, devices):
+    before, after = (value.shape[:dim], value.shape[dim + 1 :])
+    return jnp.moveaxis(value.reshape(*before, devices, -1, *after), dim, 0)
+
+
+def joined_along(blocks, dim):
+    blocks = jnp.moveaxis(blocks, 0, dim)
+    dims = blocks.shape
+    return blocks.reshape(*dims[:dim], dims[dim] * dims[dim + 1], *dims[dim + 2 :])
 
 
 def rms_scale(values):
@@ -55,13 +66,15 @@
     inv_first = rms_scale(inputs)
     normed_a = (inputs * inv_first * gain_a.astype(jnp.float32)).astype(jnp.bfloat16)
     qkv_rows = jnp.dot(normed_a, full_qkv, preferred_element_type=jnp.float32).astype(jnp.bfloat16)
-    head_rows = lax.all_to_all(
-        qkv_rows.reshape(row_count, 3, seq_count, -1),
-        "seq",
-        split_axis=2,
-        concat_axis=0,
-        tiled=True,
-    )
+    shard = qkv_rows.reshape(row_count, 3, seq_count, -1)
+    length, index = (lax.axis_size("seq"), lax.axis_index("seq"))
+    tiles = cut_along(shard, 2, length)
+    outs = [tiles[index]]
+    for step in range(1, length):
+        sent = tiles[index ^ step]
+        outs.append(lax.ppermute(sent, "seq", [(i, i ^ step) for i in range(length)]))
+    tiles = jnp.stack(outs)[index ^ jnp.arange(length)]
+    head_rows = joined_along(tiles, 0)
     head_rows = head_rows.reshape(group_len, 3, head_local, HEAD_DIM)
     position = jnp.arange(group_len, dtype=jnp.int32)
     dealt_pos = permutation[0]

time: 1140 us -> 1140 us (level)
    another operation x2 -> x6, local copies, waits for them, and re-layouts: 2.15 us -> 32.8 us  [the longest x2 17.8 us: on_device(): head_rows = head_rows.reshape(group_len, 3, head_local, HEAD_DIM)]
    reshape x4 -> x0, local copies, waits for them, and re-layouts: 27.5 us -> none  [the longest x2 17.8 us: on_device(): head_rows = head_rows.reshape(group_len, 3, head_local, HEAD_DIM)]
    all_to_all x1 -> x0, waiting for transfers between devices: 23.5 us -> none  [on_device(): lax.all_to_all(qkv_rows.reshape(row_count, 3, seq_count, -1), 'seq', spli...]
    ppermute x0 -> x3, waiting for transfers between devices: none -> 22 us  [on_device(): lax.ppermute(sent, 'seq', [(i, i ^ step) for i in range(length)])]
    unnamed x85 -> x93, local copies, waits for them, and re-layouts: 44.8 us -> 48.1 us
  transfers between devices with their start and end apart: 12 -> 14, of which waited for: 8 -> 10; matrix products, arithmetic and copies ran while one was open for 51% -> 52% of each run, Pallas kernels for 0% -> 0%
where the time goes in v1:
time: 1140 us; the launch traced here: 1130 us
  waiting for transfers between devices  363 us (32%)
  matrix products  304 us (27%)
  local copies, waits for them, and re-layouts  216 us (19%)
  other arithmetic  118 us (10%)
  blocking collectives  98 us (9%)
  between operations  15.4 us (1%)
  starting transfers between devices  11.7 us (1%)
    reduce_scatter x1, waiting for transfers between devices, on_device(): lax.psum_scatter(grad_gate_up_term.astype(jnp.bfloat16), 'fsdp', scatter_...  169 us
    psum x1, waiting for transfers between devices, on_device(): lax.psum(mlp_shards[2].astype(jnp.bfloat16), 'seq').astype(jnp.float32)  59.8 us
    all_to_all x1, blocking collectives, on_device(): lax.all_to_all(dealt_grad.reshape(group_len, 3, 1, -1), 'seq', split_axis...  51.6 us
    dot_general x4, matrix products, backward_block(): jnp.einsum('qhd,khd->hqk', grad_blk, values, preferred_element_type=jnp.f...  49.2 us
    unnamed x93, local copies, waits for them, and re-layouts  48.1 us
    all_gather x1, waiting for transfers between devices, on_device(): lax.all_gather(weight_qkv.astype(jnp.bfloat16), 'fsdp', axis=0, tiled=True)  46.5 us
    reduce_scatter x1, waiting for transfers between devices, on_device(): lax.psum_scatter(grad_qkv_term.astype(jnp.bfloat16), 'fsdp', scatter_dime...  45.8 us
    convert_element_type x4, other arithmetic, backward_block(): grad_score = (probability * (grad_prob - row_delta)).astype(jnp.bfloat16)  43.6 us
  transfers between devices with their start and end apart: 14, of which 10 were waited for; matrix products, arithmetic and copies ran while one was open for 52% of the time, Pallas kernels for 0%

profile of v1, /device:TPU:0, one launch (start us, length us, event | category | flops | bytes accessed | tf_op | source)
XLA Modules:
  0.0 1127.0 jit_solution(11109075200556743647)
XLA Ops:
  16.7 13.5 %all-gather = bf16[8,1,128]{2,1,0:T(2,128)(2,1)S(1)} all-gather(bf16[1,1,128]{2,1,0:T(2,128)(2,1)S(1)} %convert_bitcast_fusion.3), channel_id=1, replica_groups=mesh['seq'=4,'fsdp'=8] {'fsdp'}, dimensions={0}, use_global_device_ids=true | all-gather | bytes 2304 | tf_op jit(solution)/shard_map/all_gather | solution.py:62
  31.2 46.5 %all-gather.7.cloned.1.call-done = bf16[1024,3072]{1,0:T(8,128)(2,1)} async-done(((bf16[128,3072]{1,0:T(8,128)(2,1)}), bf16[1024,3072]{1,0:T(8,128)(2,1)}) %all-gather.7.cloned.1.call-update) | async-done | bytes 6291472 | tf_op jit(solution)/shard_map/all_gather | solution.py:63
  120.8 16.1 %collective-permute-done.1 = bf16[512,3,1,256]{3,0,1,2:T(8,128)(2,1)S(1)} collective-permute-done((bf16[512,3,1,256]{3,0,1,2:T(8,128)(2,1)}, bf16[512,3,1,256]{3,0,1,2:T(8,128)(2,1)S(1)}, u32[]{:S(2)}, u32[]{:S(2)}) %collective-permute-start.1) | collective-permute-done | bytes 786464 | tf_op jit(solution)/shard_map/ppermute | solution.py:75
  147.4 13.1 %reshape.405 = bf16[2048,3,4,64]{3,2,1,0:T(4,128)(2,1)} reshape(bf16[4,512,3,256]{3,2,1,0:T(4,128)(2,1)} %copy.173) | data formatting | bytes 6291456 | tf_op jit(solution)/shard_map/reshape;reshape | solution.py:78
  160.5 23.1 %gather_fusion.1 = bf16[2048,3,4,64]{3,2,1,0:T(4,128)(2,1)} fusion(bf16[2048,3,4,64]{3,2,1,0:T(4,128)(2,1)} %reshape.405, s32[2048]{0:T(1024)S(1)} %fusion.84), kind=kCustom, calls=%fused_computation.1 | custom fusion | bytes 6299648 | tf_op jit(solution)/shard_map/gather | solution.py:82
  198.9 64.4 %while.28 = (s32[]{:T(128)}, bf16[4,512,4,64]{1,3,2,0:T(8,128)(2,1)}, f32[4,4,512]{2,1,0:T(4,128)}, s32[4,512]{1,0:T(4,128)}, s32[2048]{0:T(1024)S(1)}, /*index=...) while((s32[]{:T(128)}, ...), condition=%wide.region_6.7_spmd.clone, body=%wide.region_3.6_spmd.clone.sunk | while | flops 1127348224 | bytes 57233532 | solution.py:116
  318.0 18.7 %fusion.90 = f32[512,8192]{1,0:T(8,128)} fusion(bf16[1024,8192]{1,0:T(8,128)(2,1)} %all-gather.11.cloned.1.call-done, f32[512,1024]{1,0:T(8,128)} %get-tuple-element.426, f32[1024]{0:T(1024)S(1)} %bitcast.256, f32[512]{0:T(512)S(1)} %get-tuple-element.424), kind=kOutput, calls=%fused_computation.152 | convolution fusion | flops 8591507456 | bytes 35657728 | tf_op jit(solution)/shard_map/dot_general | solution.py:129
  341.8 15.1 %multiply_convert_fusion.2 = (bf16[512,4096]{1,0:T(8,128)(2,1)}, bf16[512,4096]{1,0:T(8,128)(2,1)}, bf16[512,4096]{1,0:T(8,128)(2,1)S(1)}) fusion(f32[512,8192]{1,0:T(8,128)} %fusion.90, bf16[1024,4096]{1,0:T(8,128)(2,1)} %all-gather.13.cloned.1.call-done, bf16[1,512,1024]{2,1,0:T(8,128)(2,1)S(1)} %copy-done.24), kind=kOutput, calls=%fused_computation.68 | convolution fusion | flops 4326424576 | bytes 38797312 | tf_op jit(solution)/shard_map/dot_general | solution.py:148
  365.7 11.7 %copy.183 = bf16[1024,4096]{1,0:T(8,128)(2,1)} copy(bf16[1024,4096]{0,1:T(8,128)(2,1)} %convert_bitcast_fusion) | data formatting | bytes 16777216
  377.4 18.3 %multiply_reduce_fusion.1 = (bf16[1024]{0:T(1024)(128)(2,1)}, f32[512]{0:T(512)S(1)}, f32[512,1024]{1,0:T(8,128)}) fusion(f32[512,1024]{1,0:T(8,128)} %get-tuple-element.426, f32[512]{0:T(512)S(1)} %get-tuple-element.424, f32[1024]{0:T(1024)S(1)} %bitcast.257, bf16[1024,8192]{1,0:T(8,128)(2,1)} %all-gather.11.cloned.1.call-done, ...), kind=kOutput, calls=%fused_computation.99 | convolution fusion | flops 8609855488 | bytes 29370368 | tf_op jit(solution)/shard_map/rf,df->rd/dot_general | solution.py:155
  424.8 16.0 %gather_fusion.3 = bf16[2048,4,64]{2,1,0:T(4,128)(2,1)} fusion(bf16[2048,4,64]{2,1,0:T(4,128)(2,1)} %reshape.407, s32[2048]{0:T(1024)S(1)} %copy-done.29), kind=kCustom, calls=%fused_computation.3 | custom fusion | bytes 2105344 | tf_op jit(solution)/shard_map/gather | solution.py:175
  445.9 208.8 %while.29 = (s32[]{:T(128)}, f32[2048,4,64]{0,2,1:T(8,128)}, f32[2048,4,64]{0,2,1:T(8,128)}, bf16[4,512,4,64]{1,3,2,0:T(8,128)(2,1)}, bf16[4,512,4,64]{1,3,2,0:T...) while((s32[]{:T(128)}, f32[2048,4,64]{0,2,1:T(8,128)}, ...), condition=%wide.region_11.12_spmd.clone, body=%wide.region_9.11_spmd.clone.sunk | while | flops 2753296384 | bytes 268841472 | solution.py:209
  453.9 12.3 %multiply_reduce_fusion.5 = (f32[4,512]{1,0:T(4,128)}, f32[4,512,2048]{2,1,0:T(8,128)}) fusion(f32[4,512,2048]{2,1,0:T(8,128)S(1)} %fusion.147, f32[4,512]{1,0:T(4,128)S(1)} %dynamic-slice_bitcast_fusion.2, pred[512,2048]{1,0:T(8,128)(4,1)S(1)} %fusion.148, bf16[2048,4,64]{0,2,1:T(8,128)(2,1)} %get-tuple-element.642, ...), kind=kOutput, calls=%fused_computation.29.clone.1 | convolution fusion | flops 557840384 | bytes 35930116 | tf_op jit(solution)/shard_map/while/body/eval_jaxpr/qhd,khd->hqk/dot_general | solution.py:188
  466.2 10.9 multiply_convert_fusion.8
  505.8 12.3 %multiply_reduce_fusion.5 = (f32[4,512]{1,0:T(4,128)}, f32[4,512,2048]{2,1,0:T(8,128)}) fusion(f32[4,512,2048]{2,1,0:T(8,128)S(1)} %fusion.147, f32[4,512]{1,0:T(4,128)S(1)} %dynamic-slice_bitcast_fusion.2, pred[512,2048]{1,0:T(8,128)(4,1)S(1)} %fusion.148, bf16[2048,4,64]{0,2,1:T(8,128)(2,1)} %get-tuple-element.642, ...), kind=kOutput, calls=%fused_computation.29.clone.1 | convolution fusion | flops 557840384 | bytes 35930116 | tf_op jit(solution)/shard_map/while/body/eval_jaxpr/qhd,khd->hqk/dot_general | solution.py:188
  558.0 12.3 %multiply_reduce_fusion.5 = (f32[4,512]{1,0:T(4,128)}, f32[4,512,2048]{2,1,0:T(8,128)}) fusion(f32[4,512,2048]{2,1,0:T(8,128)S(1)} %fusion.147, f32[4,512]{1,0:T(4,128)S(1)} %dynamic-slice_bitcast_fusion.2, pred[512,2048]{1,0:T(8,128)(4,1)S(1)} %fusion.148, bf16[2048,4,64]{0,2,1:T(8,128)(2,1)} %get-tuple-element.642, ...), kind=kOutput, calls=%fused_computation.29.clone.1 | convolution fusion | flops 557840384 | bytes 35930116 | tf_op jit(solution)/shard_map/while/body/eval_jaxpr/qhd,khd->hqk/dot_general | solution.py:188
  610.2 12.3 %multiply_reduce_fusion.5 = (f32[4,512]{1,0:T(4,128)}, f32[4,512,2048]{2,1,0:T(8,128)}) fusion(f32[4,512,2048]{2,1,0:T(8,128)S(1)} %fusion.147, f32[4,512]{1,0:T(4,128)S(1)} %dynamic-slice_bitcast_fusion.2, pred[512,2048]{1,0:T(8,128)(4,1)S(1)} %fusion.148, bf16[2048,4,64]{0,2,1:T(8,128)(2,1)} %get-tuple-element.642, ...), kind=kOutput, calls=%fused_computation.29.clone.1 | convolution fusion | flops 557840384 | bytes 35930116 | tf_op jit(solution)/shard_map/while/body/eval_jaxpr/qhd,khd->hqk/dot_general | solution.py:188
  686.3 18.7 %gather_fusion.4 = bf16[2048,3,256]{2,1,0:T(4,128)(2,1)} fusion(bf16[2048,3,256]{2,1,0:T(4,128)(2,1)} %pad_maximum_fusion.3, s32[2048]{0:T(1024)S(1)} %copy-done.27), kind=kCustom, calls=%fused_computation.4 | custom fusion | bytes 6299648 | tf_op jit(solution)/shard_map/gather | solution.py:222
  705.0 51.6 %all_to_all.45 = bf16[2048,3,1,256]{3,1,2,0:T(4,128)(2,1)S(1)} all-to-all(bf16[2048,3,1,256]{3,1,2,0:T(4,128)(2,1)} %bitcast.233), channel_id=1, replica_groups=mesh['seq'=4,'fsdp'=8] {'seq'}, dimensions={0} | all-to-all | bytes 6291456 | tf_op jit(solution)/shard_map/all_to_all | solution.py:223
  770.0 16.7 %convolution_convert_fusion = bf16[1024,8192]{1,0:T(8,128)(2,1)} fusion(bf16[512,4096]{1,0:T(8,128)(2,1)} %get-tuple-element.412, bf16[512,4096]{1,0:T(8,128)(2,1)} %get-tuple-element.411, f32[512,1024]{1,0:T(8,128)S(1)} %copy-done.12, f32[1024]{0:T(1024)S(1)} %bitcast.259, f32[512]{0:T(512)S(1)} %copy-done.38), kind=kOutput, calls=%fused_computation.64 | convolution fusion | flops 8616673280 | bytes 27269120 | tf_op jit(solution)/shard_map/rd,rf->df/dot_general | solution.py:152
  789.3 45.8 %reduce-scatter.7.cloned.1.call-done = bf16[128,3072]{1,0:T(8,128)(2,1)} async-done(((bf16[1024,3072]{1,0:T(8,128)(2,1)}), bf16[128,3072]{1,0:T(8,128)(2,1)}) %reduce-scatter.7.cloned.1.call-update) | async-done | bytes 786448 | tf_op jit(solution)/shard_map/reduce_scatter | solution.py:236
  835.1 169.0 %reduce-scatter.11.cloned.1.call-done = bf16[128,8192]{1,0:T(8,128)(2,1)} async-done(((bf16[1024,8192]{1,0:T(8,128)(2,1)}), bf16[128,8192]{1,0:T(8,128)(2,1)}) %reduce-scatter.11.cloned.1.call-update) | async-done | bytes 2097168 | tf_op jit(solution)/shard_map/reduce_scatter | solution.py:247
  1023.6 13.6 %all-reduce.2 = (bf16[1024]{0:T(1024)(128)(2,1)S(1)}, bf16[1024]{0:T(1024)(128)(2,1)S(1)}) all-reduce(bf16[1024]{0:T(1024)(128)(2,1)S(1)} %get-tuple-element.351, bf16[1024]{0:T(1024)(128)(2,1)S(1)} %copy-done.40), channel_id=2, replica_groups=mesh['seq'=4,'fsdp'=8] {'fsdp'}, use_global_device_ids=true, to_apply=%region_14.15.clone | all-reduce | flops 2048 | bytes 8192
  1051.7 59.8 %all-reduce.7.cloned.1.call-done = (bf16[128,4096]{0,1:T(8,128)(2,1)}, bf16[128,3072]{1,0:T(8,128)(2,1)}, bf16[128,1024]{1,0:T(8,128)(2,1)}, bf16[128,8192]{1,0:T(8,128)(2,1)}) async-done(((bf16[128,4096]{0,1:T(8,128)(2,1)}, bf16[128,3072]{1,0:T(8,128)(2,1)}, bf16[128,1024]{1,0:T(8,128)(2,1)}, bf16[128,8192]{1,0:T(8,128)(2,1)}), (bf16[128,4096]{0,1:T(8,128)(2,1)}, bf16[128,3072]{1,0:T(8,128)(2,1)}, ...) | async-done | bytes 4194320 | tf_op jit(solution)/shard_map/psum | solution.py:260
  (341 shorter events, 482.8 us)
Async XLA Ops:
  7.2 70.6 %all-gather.7.cloned.1.call-start = ((), (), s32[]{:S(2)}) async-start(), calls=%async_computation.7 | async-start | bytes 7077888 | tf_op jit(solution)/shard_map/all_gather | solution.py:63
  9.6 303.8 %all-gather.9.cloned.1.call-start = ((), (), s32[]{:S(2)}) async-start(), calls=%async_computation.8 | async-start | bytes 2359296 | tf_op jit(solution)/shard_map/all_gather | solution.py:64
  11.5 306.5 %all-gather.11.cloned.1.call-start = ((), (), s32[]{:S(2)}) async-start(), calls=%async_computation.9 | async-start | bytes 18874368 | tf_op jit(solution)/shard_map/all_gather | solution.py:124
  15.5 326.3 %all-gather.13.cloned.1.call-start = ((), (), s32[]{:S(2)}) async-start(), calls=%async_computation.10 | async-start | bytes 9437184 | tf_op jit(solution)/shard_map/all_gather | solution.py:125
  30.2 47.5 %copy-start.32 = (f32[8,1,128]{2,1,0:T(1,128)}, f32[8,1,128]{2,1,0:T(1,128)S(1)}, u32[]{:S(2)}) copy-start(f32[8,1,128]{2,1,0:T(1,128)S(1)} %convert_element_type.214) | copy-start | bytes 12292
  31.1 46.6 %copy-start.35 = (f32[512]{0:T(512)}, f32[512]{0:T(512)S(1)}, u32[]{:S(2)}) copy-start(f32[512]{0:T(512)S(1)} %get-tuple-element.422) | copy-start | bytes 6148
  98.3 16.7 %copy-start.14 = (bf16[512,3,1,1,256]{4,2,1,0,3:T(2,128)(2,1)S(1)}, bf16[512,3,1,1,256]{4,2,1,0,3:T(2,128)(2,1)}, u32[]{:S(2)}) copy-start(bf16[512,3,1,1,256]{4,2,1,0,3:T(2,128)(2,1)} %get-tuple-element.417) | copy-start | bytes 2359300
  99.3 21.5 %collective-permute-start.2 = (bf16[512,3,1,256]{3,0,1,2:T(8,128)(2,1)}, bf16[512,3,1,256]{3,0,1,2:T(8,128)(2,1)S(1)}, u32[]{:S(2)}, u32[]{:S(2)}) collective-permute-start(bf16[512,3,1,256]{3,0,1,2:T(8,128)(2,1)} %bitcast.183), channel_id=1, source_target_pairs={{0,24},{8,16},{16,8},{24,0},{1,25},{9,17},{17,9},{25,1},{2,26},{10... | collective-permute-start | bytes 2359304 | tf_op jit(solution)/shard_map/ppermute | solution.py:75
  102.7 34.3 %collective-permute-start.1 = (bf16[512,3,1,256]{3,0,1,2:T(8,128)(2,1)}, bf16[512,3,1,256]{3,0,1,2:T(8,128)(2,1)S(1)}, u32[]{:S(2)}, u32[]{:S(2)}) collective-permute-start(bf16[512,3,1,256]{3,0,1,2:T(8,128)(2,1)} %bitcast.184), channel_id=1, source_target_pairs={{0,16},{8,24},{16,0},{24,8},{1,17},{9,25},{17,1},{25,9},{2,18},{10... | collective-permute-start | bytes 2359304 | tf_op jit(solution)/shard_map/ppermute | solution.py:75
  104.3 32.8 %collective-permute-start = (bf16[512,3,1,256]{3,0,1,2:T(8,128)(2,1)}, bf16[512,3,1,256]{3,0,1,2:T(8,128)(2,1)}, u32[]{:S(2)}, u32[]{:S(2)}) collective-permute-start(bf16[512,3,1,256]{3,0,1,2:T(8,128)(2,1)} %bitcast.185), channel_id=1, source_target_pairs={{0,8},{8,0},{16,24},{24,16},{1,9},{9,1},{17,25},{25,17},{2,10},{10... | collective-permute-start | bytes 2359304 | tf_op jit(solution)/shard_map/ppermute | solution.py:75
  115.0 45.5 %copy-start.28 = (s32[2048]{0:T(1024)}, s32[2048]{0:T(1024)S(1)}, u32[]{:S(2)}) copy-start(s32[2048]{0:T(1024)S(1)} %fusion.84) | copy-start | bytes 24580
  286.0 18.1 %all-to-all-start = ((bf16[4,2,65536]{2,1,0:T(2,128)(2,1)}), bf16[4,2,65536]{2,1,0:T(2,128)(2,1)}, u32[]{:S(2)}, u32[]{:S(2)}) async-start(bf16[4,2,65536]{2,1,0:T(2,128)(2,1)} %reshape.418), calls=%async_computation | async-start | bytes 2097152 | tf_op jit(solution)/shard_map/all_to_all | solution.py:118
  290.3 496.5 %reduce-scatter.13.cloned.1.call-start = ((), (), s32[]{:S(2)}) async-start(), calls=%async_computation.14 | async-start | bytes 9437184
  299.5 96.2 %copy-start.30 = (f32[8,1,128]{2,1,0:T(1,128)}, f32[8,1,128]{2,1,0:T(1,128)S(1)}, u32[]{:S(2)}) copy-start(f32[8,1,128]{2,1,0:T(1,128)S(1)} %convert_element_type.215) | copy-start | bytes 12292
  318.0 77.7 %copy-start.37 = (f32[512]{0:T(512)}, f32[512]{0:T(512)S(1)}, u32[]{:S(2)}) copy-start(f32[512]{0:T(512)S(1)} %get-tuple-element.424) | copy-start | bytes 6148
  318.0 23.7 %copy-start.24 = (bf16[1,512,1024]{2,1,0:T(8,128)(2,1)S(1)}, bf16[1,512,1024]{2,1,0:T(8,128)(2,1)}, u32[]{:S(2)}) copy-start(bf16[1,512,1024]{2,1,0:T(8,128)(2,1)} %param.22) | copy-start | bytes 3145732
  402.6 17.9 %all-to-all-start.1 = ((bf16[512,4,256]{0,2,1:T(8,128)(2,1)}), bf16[512,4,256]{0,2,1:T(8,128)(2,1)S(1)}, u32[]{:S(2)}, u32[]{:S(2)}) async-start(bf16[512,4,256]{0,2,1:T(8,128)(2,1)} %bitcast.241), calls=%async_computation.1 | async-start | bytes 2097152 | tf_op jit(solution)/shard_map/all_to_all | solution.py:172
  406.3 383.0 %reduce-scatter.9.cloned.1.call-start = ((), (), s32[]{:S(2)}) async-start(), calls=%async_computation.12 | async-start | bytes 2359296 | tf_op jit(solution)/shard_map/reduce_scatter | solution.py:239
  410.8 424.2 %reduce-scatter.7.cloned.1.call-start = ((), (), s32[]{:S(2)}) async-start(), calls=%async_computation.11 | async-start | bytes 7077888 | tf_op jit(solution)/shard_map/reduce_scatter | solution.py:236
  768.4 235.6 %reduce-scatter.11.cloned.1.call-start = ((), (), s32[]{:S(2)}) async-start(), calls=%async_computation.13 | async-start | bytes 18874368 | tf_op jit(solution)/shard_map/reduce_scatter | solution.py:247
  786.7 217.4 %copy-start.45 = (u32[32]{0:T(128)S(1)}, u32[32]{0:T(128)}, u32[]{:S(2)}) copy-start(u32[32]{0:T(128)} %constant.88) | copy-start | bytes 388
  786.7 324.9 %all-reduce.7.cloned.1.call-start = ((), (), s32[]{:S(2)}) async-start(), calls=%async_computation.15 | async-start | bytes 8388608 | tf_op jit(solution)/shard_map/psum | solution.py:260
  1015.6 33.0 %copy-start.11 = (f32[512,1024]{1,0:T(8,128)S(1)}, f32[512,1024]{1,0:T(8,128)}, u32[]{:S(2)}) copy-start(f32[512,1024]{1,0:T(8,128)} %copy-done.10) | copy-start | bytes 6291460
  1015.7 33.0 %copy-start.34 = (f32[512]{0:T(512)S(1)}, f32[512]{0:T(512)}, u32[]{:S(2)}) copy-start(f32[512]{0:T(512)} %get-tuple-element.421) | copy-start | bytes 6148
  (72 other events, 513.5 us)
Sparse Core Ops, SparseCore 0:
  10.2 67.4 all-gather.6
  79.9 27.7 all-gather.8
  109.3 150.5 all-gather.10
  261.4 80.3 all-gather.12
  377.5 88.0 reduce-scatter.12
  467.8 34.1 reduce-scatter.8
  768.5 66.4 reduce-scatter.6
  837.4 166.5 reduce-scatter.10
  1008.3 103.2 all-reduce.6
